TPU v7x, 128 devices: a whole 4x4x4 slice. The times are simulated.
128 devices in a mesh: row: 8 (over z, core), col: 16 (over y, x).
Axes of the slice: x: 4, y: 4, z: 4, core: 2. Of those that a mesh axis runs over, the one named last changes fastest.
Arguments:
- front_diag: float32 [1024, 1024], replicated, may hold values from -4 to 16, as said below
- panel_rows: float32 [16384, 1024], P(('row', 'col')), may hold values from -1.2 to 1.2
- trailing: float32 [16384, 16384], P('row', 'col'), may hold values from -6 to 6
- pattern: int32 [64, 64], P('row', 'col'), may hold values 0 or 1
Outputs:
- diag_factor: float32 [1024, 1024], replicated
- panel_factor: float32 [16384, 1024], P(('row', 'col'))
- schur: float32 [16384, 16384], P('row', 'col')
Inputs may be any that keep to these rules, and one draw needn't show every extreme that they name: front_diag is symmetric and positive definite, with smallest eigenvalue at least 0.5.
All inputs are finite; a program needn't handle non-finite values. No bound on the sum of `pattern` on one device may be relied on, other than what follows from the above.
Results may differ from a plain program's by a relative error of at most 0.0003.
Values sent between devices are 32-bit elements; how exact they have to be, the bound alone decides.
A program may use at most 128 MiB of HBM per device.

v0:
```python
import jax
import jax.numpy as jnp
from jax import lax
from jax.sharding import PartitionSpec as P

BLOCK = 256


def spread(block, axis, holder):
    block = jnp.where(lax.axis_index(axis) == holder, block, jnp.zeros_like(block))
    return lax.psum(block, axis)


def column_rows(row_part, col_rows):
    ratio = lax.axis_size("col") // lax.axis_size("row")
    offset = lax.axis_index("col") % ratio * col_rows
    return lax.dynamic_slice_in_dim(row_part, offset, col_rows, 0)


def local(front_diag, panel_rows, trailing, pattern):
    diag_factor = jnp.linalg.cholesky(front_diag)
    panel_factor = jax.scipy.linalg.solve_triangular(diag_factor, panel_rows.T, lower=True).T
    local_rows = trailing.shape[0]
    col_rows = trailing.shape[1]
    ratio = lax.axis_size("col") // lax.axis_size("row")
    root_row = lax.axis_index("col") // ratio
    row_part = lax.all_gather(panel_factor, "col", axis=0, tiled=True)
    piece = column_rows(row_part, col_rows)
    col_part = spread(piece, "row", root_row)
    update = jnp.dot(row_part, col_part.T, precision=lax.Precision.HIGHEST)
    row_blocks = local_rows // BLOCK
    col_blocks = col_rows // BLOCK
    row_index = lax.axis_index("row") * row_blocks + jnp.arange(row_blocks)
    col_index = lax.axis_index("col") * col_blocks + jnp.arange(col_blocks)
    lower = (row_index[:, None] >= col_index[None, :]).astype(jnp.float32)
    keep = pattern.astype(jnp.float32) * lower
    masked = update.reshape(row_blocks, BLOCK, col_blocks, BLOCK) * keep[:, None, :, None]
    schur = trailing - masked.reshape(local_rows, col_rows)
    return (diag_factor, panel_factor, schur)


def solution(mesh):
    return jax.shard_map(
        local,
        mesh=mesh,
        in_specs=(P(), P(("row", "col"), None), P("row", "col"), P("row", "col")),
        out_specs=(P(), P(("row", "col"), None), P("row", "col")),
        check_vma=False,
    )
```

profile of v0, /device:TPU:0, one launch (start us, length us, event | category | flops | bytes accessed | tf_op | source)
XLA Modules:
  0.0 537.7 jit_solution(12177218288238149050)
XLA Ops:
  7.2 5.3 copy.7
  12.6 4.4 fusion
  19.0 11.7 %cholesky.223 = f32[128,128]{1,0:T(8,128)S(1)} custom-call(f32[128,128]{1,0:T(8,128)S(1)} %cholesky.580), custom_call_target="Cholesky" | custom-call | tf_op jit(solution)/shard_map/jit(cholesky)/cholesky | solution.py:21
  30.8 9.8 %custom-call.63 = f32[1,128,128]{1,2,0:T(8,128)S(1)} custom-call(f32[1,128,128]{2,1,0:T(8,128)S(1)} %get-tuple-element.61), custom_call_target="InvertDiagBlocksLowerTriangular" | custom-call | tf_op jit(solution)/shard_map/jit(cholesky)/cholesky | solution.py:21
  40.6 2.5 cholesky.255
  43.1 2.3 constant_dynamic-update-slice_fusion.32
  47.0 11.9 %cholesky.244 = f32[128,128]{1,0:T(8,128)S(1)} custom-call(f32[128,128]{1,0:T(8,128)S(1)} %cholesky.584), custom_call_target="Cholesky" | custom-call | tf_op jit(solution)/shard_map/jit(cholesky)/cholesky | solution.py:21
  59.5 9.8 %custom-call.64 = f32[1,128,128]{1,2,0:T(8,128)S(1)} custom-call(f32[1,128,128]{2,1,0:T(8,128)S(1)} %get-tuple-element.58), custom_call_target="InvertDiagBlocksLowerTriangular" | custom-call | tf_op jit(solution)/shard_map/jit(cholesky)/cholesky | solution.py:21
  72.7 11.7 %cholesky.468 = f32[128,128]{1,0:T(8,128)S(1)} custom-call(f32[128,128]{1,0:T(8,128)S(1)} %cholesky.589), custom_call_target="Cholesky" | custom-call | tf_op jit(solution)/shard_map/jit(cholesky)/cholesky | solution.py:21
  85.7 9.8 %custom-call.65 = f32[1,128,128]{1,2,0:T(8,128)S(1)} custom-call(f32[1,128,128]{2,1,0:T(8,128)S(1)} %get-tuple-element.55), custom_call_target="InvertDiagBlocksLowerTriangular" | custom-call | tf_op jit(solution)/shard_map/jit(cholesky)/cholesky | solution.py:21
  96.6 2.3 convolution_subtract_fusion.2
  99.0 11.9 %cholesky.487 = f32[128,128]{1,0:T(8,128)S(1)} custom-call(f32[128,128]{1,0:T(8,128)S(1)} %cholesky.594), custom_call_target="Cholesky" | custom-call | tf_op jit(solution)/shard_map/jit(cholesky)/cholesky | solution.py:21
  112.2 9.8 %custom-call.66 = f32[1,128,128]{1,2,0:T(8,128)S(1)} custom-call(f32[1,128,128]{2,1,0:T(8,128)S(1)} %get-tuple-element.52), custom_call_target="InvertDiagBlocksLowerTriangular" | custom-call | tf_op jit(solution)/shard_map/jit(cholesky)/cholesky | solution.py:21
  123.1 2.4 convolution_subtract_fusion.3
  125.4 11.7 %cholesky.506 = f32[128,128]{1,0:T(8,128)S(1)} custom-call(f32[128,128]{1,0:T(8,128)S(1)} %cholesky.599), custom_call_target="Cholesky" | custom-call | tf_op jit(solution)/shard_map/jit(cholesky)/cholesky | solution.py:21
  138.5 10.2 %custom-call.67 = f32[1,128,128]{1,2,0:T(8,128)S(1)} custom-call(f32[1,128,128]{2,1,0:T(8,128)S(1)} %get-tuple-element.49), custom_call_target="InvertDiagBlocksLowerTriangular" | custom-call | tf_op jit(solution)/shard_map/jit(cholesky)/cholesky | solution.py:21
  149.7 2.3 convolution_subtract_fusion.4
  152.0 11.7 %cholesky.526 = f32[128,128]{1,0:T(8,128)S(1)} custom-call(f32[128,128]{1,0:T(8,128)S(1)} %cholesky.604), custom_call_target="Cholesky" | custom-call | tf_op jit(solution)/shard_map/jit(cholesky)/cholesky | solution.py:21
  165.0 9.8 %custom-call.68 = f32[1,128,128]{1,2,0:T(8,128)S(1)} custom-call(f32[1,128,128]{2,1,0:T(8,128)S(1)} %get-tuple-element.46), custom_call_target="InvertDiagBlocksLowerTriangular" | custom-call | tf_op jit(solution)/shard_map/jit(cholesky)/cholesky | solution.py:21
  177.9 11.9 %cholesky.546 = f32[128,128]{1,0:T(8,128)S(1)} custom-call(f32[128,128]{1,0:T(8,128)S(1)} %cholesky.609), custom_call_target="Cholesky" | custom-call | tf_op jit(solution)/shard_map/jit(cholesky)/cholesky | solution.py:21
  191.0 9.8 %custom-call.69 = f32[1,128,128]{1,2,0:T(8,128)S(1)} custom-call(f32[1,128,128]{2,1,0:T(8,128)S(1)} %get-tuple-element.43), custom_call_target="InvertDiagBlocksLowerTriangular" | custom-call | tf_op jit(solution)/shard_map/jit(cholesky)/cholesky | solution.py:21
  203.4 11.7 %cholesky.564 = f32[128,128]{1,0:T(8,128)S(1)} custom-call(f32[128,128]{1,0:T(8,128)S(1)} %convolution_subtract_fusion.11), custom_call_target="Cholesky" | custom-call | tf_op jit(solution)/shard_map/jit(cholesky)/cholesky | solution.py:21
  222.0 6.8 %fusion.1 = (f32[1024,1024]{1,0:T(8,128)}, f32[1024,1024]{1,0:T(8,128)}) fusion(f32[1024,1024]{1,0:T(8,128)} %get-tuple-element.41, pred[]{:T(512)S(6)} %cholesky.579), kind=kLoop, calls=%fused_computation.8 | loop fusion | flops 4194304 | bytes 12582913 | tf_op jit(solution)/shard_map/jit(_solve_triangular)/triangular_solve | solution.py:22
  228.8 22.5 %while.1 = (s32[]{:T(128)}, f32[1024,1024]{1,0:T(8,128)}, s32[8,2]{0,1:T(2,128)S(1)}, f32[8,128,128]{2,1,0:T(8,128)S(1)}, s32[]{:T(128)}) while((s32[]{:T(128)}, f32[1024,1024]{1,0:T(8,128)}, s32[8,2]{0,1:T(2,128)S(1)}, f32[8,128,128]{2,1,0:T(8,128)S(1)}, s32[]{:T(128)}) %tuple.58), condition=%wide.while_cond, body=%wide.while_body.sunk | while | flops 2 | bytes 131189 | solution.py:22
  229.4 2.2 bitcast_dynamic-update-slice_fusion.2
  232.3 2.2 bitcast_dynamic-update-slice_fusion.2
  251.3 78.8 %custom-call.70 = f32[8,128,128]{1,2,0:T(8,128)S(1)} custom-call(f32[8,128,128]{2,1,0:T(8,128)S(1)} %get-tuple-element.10), custom_call_target="InvertDiagBlocksLowerTriangular" | custom-call | tf_op jit(solution)/shard_map/jit(_solve_triangular)/triangular_solve | solution.py:22
  344.9 73.2 %all-gather.2.cloned.1.call-done = f32[2048,1024]{1,0:T(8,128)} async-done(((f32[128,1024]{1,0:T(8,128)}), f32[2048,1024]{1,0:T(8,128)}) %all-gather.2.cloned.1.call-update) | async-done | bytes 8388624 | tf_op jit(solution)/shard_map/all_gather | solution.py:27
  418.1 5.0 dynamic-slice_select_fusion
  425.0 5.5 %copy.18 = f32[256,8,4,256]{3,1,2,0:T(8,128)} copy(f32[256,8,4,256]{3,2,1,0:T(4,128)S(1)} %bitcast.109) | data formatting | bytes 16777216
  430.5 65.2 %all-reduce.3.cloned.1.call-done = f32[1024,1024]{1,0:T(8,128)} async-done(((f32[1024,1024]{1,0:T(8,128)}), f32[1024,1024]{1,0:T(8,128)}) %all-reduce.3.cloned.1.call-update) | async-done | bytes 4194320 | tf_op jit(solution)/shard_map/psum | solution.py:11
  495.8 34.7 %multiply_subtract_fusion = f32[2048,1024]{1,0:T(8,128)} fusion(f32[2048,1024]{1,0:T(8,128)} %param.6, f32[2048,1024]{1,0:T(8,128)} %bitcast.108, f32[2048,1024]{1,0:T(8,128)} %all-gather.2.cloned.1.call-done, f32[1024,1024]{1,0:T(8,128)} %all-reduce.3.cloned.1.call-done), kind=kOutput, calls=%fused_computation.2 | convolution fusion | flops 25773998080 | bytes 37748736 | tf_op jit(solution)/shard_map/dot_general | solution.py:30
  (103 shorter events, 59.3 us)
Async XLA Ops:
  7.2 410.9 %all-gather.2.cloned.1.call-start = ((), (), s32[]{:S(2)}) async-start(), calls=%async_computation | async-start | bytes 8912896 | tf_op jit(solution)/shard_map/all_gather | solution.py:27
  17.0 2.0 copy-start
  222.0 108.2 %copy-start.2 = (f32[128,1024]{1,0:T(8,128)S(1)}, f32[128,1024]{1,0:T(8,128)}, u32[]{:S(2)}) copy-start(f32[128,1024]{1,0:T(8,128)} %param.5) | copy-start | bytes 1572868
  344.0 0.8 copy-start.1
  344.8 150.9 %all-reduce.3.cloned.1.call-start = ((), (), s32[]{:S(2)}) async-start(), calls=%async_computation.1 | async-start | bytes 8388608 | tf_op jit(solution)/shard_map/psum | solution.py:11
  423.1 0.7 copy-start.3
Sparse Core Ops, SparseCore 0:
  345.0 73.0 all-gather.1
  423.2 72.5 all-reduce.2
where the time goes:
time: 548 us; the launch traced here: 538 us
  other arithmetic  267 us (49%)
  waiting for transfers between devices  138 us (25%)
  matrix products  70.7 us (13%)
  local copies, waits for them, and re-layouts  41.1 us (8%)
  between operations  19.9 us (4%)
    another operation x30, other arithmetic, local(): diag_factor = jnp.linalg.cholesky(front_diag)  172 us
    another operation x3, other arithmetic, local(): jax.scipy.linalg.solve_triangular(diag_factor, panel_rows.T, lower=True)  85.7 us
    all_gather x1, waiting for transfers between devices, local(): row_part = lax.all_gather(panel_factor, 'col', axis=0, tiled=True)  73.2 us
    psum x1, waiting for transfers between devices, spread(): return lax.psum(block, axis)  65.2 us
    dot_general x1, matrix products, local(): update = jnp.dot(row_part, col_part.T, precision=lax.Precision.HIGHEST)  34.7 us
    another operation x14, matrix products, local(): diag_factor = jnp.linalg.cholesky(front_diag)  23 us
    another operation x24, local copies, waits for them, and re-layouts  22.4 us
    unnamed x17, local copies, waits for them, and re-layouts  14.3 us
  transfers between devices with their start and end apart: 2, of which 2 were waited for; matrix products, arithmetic and copies ran while one was open for 1% of the time, Pallas kernels for 0%

commit v1 on v0

--- a/solution.py
+++ b/solution.py
@@ -4,6 +4,12 @@
 from jax.sharding import PartitionSpec as P
 
 BLOCK = 256
+
+
+def in_order(parts, dim):
+    dims = list(parts.shape[1:])
+    dims[dim] *= parts.shape[0]
+    return jnp.moveaxis(parts, 0, dim).reshape(dims)
 
 
 def spread(block, axis, holder):
@@ -24,7 +30,19 @@
     col_rows = trailing.shape[1]
     ratio = lax.axis_size("col") // lax.axis_size("row")
     root_row = lax.axis_index("col") // ratio
-    row_part = lax.all_gather(panel_factor, "col", axis=0, tiled=True)
+    size = lax.axis_size("col")
+    pairs = [(i, (i + 1) % size) for i in range(size)]
+    back = [(b, a) for a, b in pairs]
+    lower_2, upper = ([], [])
+    for step in range(size - 1):
+        if step % 2 == 0:
+            lower_2.append(lax.ppermute(lower_2[-1] if lower_2 else panel_factor, "col", pairs))
+        else:
+            upper.append(lax.ppermute(upper[-1] if upper else panel_factor, "col", back))
+    blocks = jnp.stack([*lower_2[::-1], panel_factor, *upper])
+    shift = lax.axis_index("col") - len(lower_2)
+    blocks = blocks[(jnp.arange(size) - shift) % size]
+    row_part = in_order(blocks, 0)
     piece = column_rows(row_part, col_rows)
     col_part = spread(piece, "row", root_row)
     update = jnp.dot(row_part, col_part.T, precision=lax.Precision.HIGHEST)

time: 548 us -> 663 us (1.21)
  local copies, waits for them, and re-layouts: 41.1 us -> 111 us
  starting transfers between devices: 0.08 us -> 40.7 us
  other arithmetic: 267 us -> 279 us
    ppermute x0 -> x15, waiting for transfers between devices: none -> 73.2 us  [the longest x8 71.1 us: local(): lax.ppermute(lower_2[-1] if lower_2 else panel_factor, 'col', pairs)]
    all_gather x1 -> x0, waiting for transfers between devices: 73.2 us -> none  [local(): row_part = lax.all_gather(panel_factor, 'col', axis=0, tiled=True)]
    unnamed x17 -> x42, local copies, waits for them, and re-layouts: 14.3 us -> 57.9 us
    ppermute x0 -> x15, starting transfers between devices: none -> 40.6 us  [the longest x7 39 us: local(): lax.ppermute(upper[-1] if upper else panel_factor, 'col', back)]
    gather x0 -> x2, local copies, waits for them, and re-layouts: none -> 16.9 us  [local(): blocks = blocks[(jnp.arange(size) - shift) % size]]
    sub x0 -> x1, other arithmetic: none -> 11.7 us  [local(): schur = trailing - masked.reshape(local_rows, col_rows)]
    mul x1, local copies, waits for them, and re-layouts: 1.15 us -> 10.6 us  [local(): update.reshape(row_blocks, BLOCK, col_blocks, BLOCK)]
    another operation x24 -> x25, local copies, waits for them, and re-layouts: 22.4 us -> 23.2 us
  transfers between devices with their start and end apart: 2 -> 16, of which waited for: 2 -> 12; matrix products, arithmetic and copies ran while one was open for 1% -> 4% of each run, Pallas kernels for 0% -> 0%
where the time goes in v1:
time: 663 us; the launch traced here: 653 us
  other arithmetic  279 us (42%)
  waiting for transfers between devices  133 us (20%)
  local copies, waits for them, and re-layouts  111 us (17%)
  matrix products  68.6 us (10%)
  starting transfers between devices  40.7 us (6%)
  between operations  19.8 us (3%)
    another operation x30, other arithmetic, local(): diag_factor = jnp.linalg.cholesky(front_diag)  172 us
    another operation x3, other arithmetic, local(): jax.scipy.linalg.solve_triangular(diag_factor, panel_rows.T, lower=True)  85.6 us
    ppermute x8, waiting for transfers between devices, local(): lax.ppermute(lower_2[-1] if lower_2 else panel_factor, 'col', pairs)  71.1 us
    psum x1, waiting for transfers between devices, spread(): return lax.psum(block, axis)  59.5 us
    unnamed x42, local copies, waits for them, and re-layouts  57.9 us
    ppermute x7, starting transfers between devices, local(): lax.ppermute(upper[-1] if upper else panel_factor, 'col', back)  39 us
    dot_general x1, matrix products, local(): update = jnp.dot(row_part, col_part.T, precision=lax.Precision.HIGHEST)  32.5 us
    another operation x14, matrix products, local(): diag_factor = jnp.linalg.cholesky(front_diag)  23 us
  transfers between devices with their start and end apart: 16, of which 12 were waited for; matrix products, arithmetic and copies ran while one was open for 4% of the time, Pallas kernels for 0%

profile of v1, /device:TPU:0, one launch (start us, length us, event | category | flops | bytes accessed | tf_op | source)
XLA Modules:
  0.0 652.6 jit_solution(5319879922713346626)
XLA Ops:
  19.0 11.7 %cholesky.223 = f32[128,128]{1,0:T(8,128)S(1)} custom-call(f32[128,128]{1,0:T(8,128)S(1)} %cholesky.580), custom_call_target="Cholesky" | custom-call | tf_op jit(solution)/shard_map/jit(cholesky)/cholesky | solution.py:27
  30.8 9.8 %custom-call.63 = f32[1,128,128]{1,2,0:T(8,128)S(1)} custom-call(f32[1,128,128]{2,1,0:T(8,128)S(1)} %get-tuple-element.75), custom_call_target="InvertDiagBlocksLowerTriangular" | custom-call | tf_op jit(solution)/shard_map/jit(cholesky)/cholesky | solution.py:27
  47.0 12.0 %cholesky.244 = f32[128,128]{1,0:T(8,128)S(1)} custom-call(f32[128,128]{1,0:T(8,128)S(1)} %cholesky.584), custom_call_target="Cholesky" | custom-call | tf_op jit(solution)/shard_map/jit(cholesky)/cholesky | solution.py:27
  59.7 9.8 %custom-call.64 = f32[1,128,128]{1,2,0:T(8,128)S(1)} custom-call(f32[1,128,128]{2,1,0:T(8,128)S(1)} %get-tuple-element.72), custom_call_target="InvertDiagBlocksLowerTriangular" | custom-call | tf_op jit(solution)/shard_map/jit(cholesky)/cholesky | solution.py:27
  72.9 11.7 %cholesky.468 = f32[128,128]{1,0:T(8,128)S(1)} custom-call(f32[128,128]{1,0:T(8,128)S(1)} %cholesky.589), custom_call_target="Cholesky" | custom-call | tf_op jit(solution)/shard_map/jit(cholesky)/cholesky | solution.py:27
  85.8 9.8 %custom-call.65 = f32[1,128,128]{1,2,0:T(8,128)S(1)} custom-call(f32[1,128,128]{2,1,0:T(8,128)S(1)} %get-tuple-element.69), custom_call_target="InvertDiagBlocksLowerTriangular" | custom-call | tf_op jit(solution)/shard_map/jit(cholesky)/cholesky | solution.py:27
  99.2 11.8 %cholesky.487 = f32[128,128]{1,0:T(8,128)S(1)} custom-call(f32[128,128]{1,0:T(8,128)S(1)} %cholesky.594), custom_call_target="Cholesky" | custom-call | tf_op jit(solution)/shard_map/jit(cholesky)/cholesky | solution.py:27
  112.3 9.8 %custom-call.66 = f32[1,128,128]{1,2,0:T(8,128)S(1)} custom-call(f32[1,128,128]{2,1,0:T(8,128)S(1)} %get-tuple-element.66), custom_call_target="InvertDiagBlocksLowerTriangular" | custom-call | tf_op jit(solution)/shard_map/jit(cholesky)/cholesky | solution.py:27
  125.6 11.7 %cholesky.506 = f32[128,128]{1,0:T(8,128)S(1)} custom-call(f32[128,128]{1,0:T(8,128)S(1)} %cholesky.599), custom_call_target="Cholesky" | custom-call | tf_op jit(solution)/shard_map/jit(cholesky)/cholesky | solution.py:27
  138.6 10.0 %custom-call.67 = f32[1,128,128]{1,2,0:T(8,128)S(1)} custom-call(f32[1,128,128]{2,1,0:T(8,128)S(1)} %get-tuple-element.63), custom_call_target="InvertDiagBlocksLowerTriangular" | custom-call | tf_op jit(solution)/shard_map/jit(cholesky)/cholesky | solution.py:27
  152.0 11.7 %cholesky.526 = f32[128,128]{1,0:T(8,128)S(1)} custom-call(f32[128,128]{1,0:T(8,128)S(1)} %cholesky.604), custom_call_target="Cholesky" | custom-call | tf_op jit(solution)/shard_map/jit(cholesky)/cholesky | solution.py:27
  165.0 9.8 %custom-call.68 = f32[1,128,128]{1,2,0:T(8,128)S(1)} custom-call(f32[1,128,128]{2,1,0:T(8,128)S(1)} %get-tuple-element.60), custom_call_target="InvertDiagBlocksLowerTriangular" | custom-call | tf_op jit(solution)/shard_map/jit(cholesky)/cholesky | solution.py:27
  177.8 12.1 %cholesky.546 = f32[128,128]{1,0:T(8,128)S(1)} custom-call(f32[128,128]{1,0:T(8,128)S(1)} %cholesky.609), custom_call_target="Cholesky" | custom-call | tf_op jit(solution)/shard_map/jit(cholesky)/cholesky | solution.py:27
  191.2 9.8 %custom-call.69 = f32[1,128,128]{1,2,0:T(8,128)S(1)} custom-call(f32[1,128,128]{2,1,0:T(8,128)S(1)} %get-tuple-element.57), custom_call_target="InvertDiagBlocksLowerTriangular" | custom-call | tf_op jit(solution)/shard_map/jit(cholesky)/cholesky | solution.py:27
  203.6 11.7 %cholesky.564 = f32[128,128]{1,0:T(8,128)S(1)} custom-call(f32[128,128]{1,0:T(8,128)S(1)} %convolution_subtract_fusion.11), custom_call_target="Cholesky" | custom-call | tf_op jit(solution)/shard_map/jit(cholesky)/cholesky | solution.py:27
  222.2 6.8 %fusion.3 = (f32[1024,1024]{1,0:T(8,128)}, f32[1024,1024]{1,0:T(8,128)}) fusion(f32[1024,1024]{1,0:T(8,128)} %get-tuple-element.55, pred[]{:T(512)S(6)} %cholesky.579), kind=kLoop, calls=%fused_computation.11 | loop fusion | flops 4194304 | bytes 12582913 | tf_op jit(solution)/shard_map/jit(_solve_triangular)/triangular_solve | solution.py:28
  229.0 22.5 %while.1 = (s32[]{:T(128)}, f32[1024,1024]{1,0:T(8,128)}, s32[8,2]{0,1:T(2,128)S(1)}, f32[8,128,128]{2,1,0:T(8,128)S(1)}, s32[]{:T(128)}) while((s32[]{:T(128)}, f32[1024,1024]{1,0:T(8,128)}, s32[8,2]{0,1:T(2,128)S(1)}, f32[8,128,128]{2,1,0:T(8,128)S(1)}, s32[]{:T(128)}) %tuple.64), condition=%wide.while_cond, body=%wide.while_body.sunk | while | flops 2 | bytes 131181 | solution.py:28
  251.5 78.8 %custom-call.70 = f32[8,128,128]{1,2,0:T(8,128)S(1)} custom-call(f32[8,128,128]{2,1,0:T(8,128)S(1)} %get-tuple-element.10), custom_call_target="InvertDiagBlocksLowerTriangular" | custom-call | tf_op jit(solution)/shard_map/jit(_solve_triangular)/triangular_solve | solution.py:28
  345.2 15.6 %collective-permute-done = f32[128,1024]{0,1:T(8,128)S(1)} collective-permute-done((f32[128,1024]{0,1:T(8,128)S(1)}, f32[128,1024]{0,1:T(8,128)S(1)}, u32[]{:S(2)}, u32[]{:S(2)}) %collective-permute-start) | collective-permute-done | bytes 524320 | tf_op jit(solution)/shard_map/ppermute | solution.py:39
  366.1 11.0 %collective-permute-done.1 = f32[128,1024]{0,1:T(8,128)S(1)} collective-permute-done((f32[128,1024]{0,1:T(8,128)S(1)}, f32[128,1024]{0,1:T(8,128)S(1)}, u32[]{:S(2)}, u32[]{:S(2)}) %collective-permute-start.1) | collective-permute-done | bytes 524320 | tf_op jit(solution)/shard_map/ppermute | solution.py:39
  382.5 10.1 %collective-permute-done.2 = f32[128,1024]{0,1:T(8,128)S(1)} collective-permute-done((f32[128,1024]{0,1:T(8,128)S(1)}, f32[128,1024]{0,1:T(8,128)S(1)}, u32[]{:S(2)}, u32[]{:S(2)}) %collective-permute-start.2) | collective-permute-done | bytes 524320 | tf_op jit(solution)/shard_map/ppermute | solution.py:39
  398.0 9.2 %collective-permute-done.3 = f32[128,1024]{0,1:T(8,128)S(1)} collective-permute-done((f32[128,1024]{0,1:T(8,128)S(1)}, f32[128,1024]{0,1:T(8,128)S(1)}, u32[]{:S(2)}, u32[]{:S(2)}) %collective-permute-start.3) | collective-permute-done | bytes 524320 | tf_op jit(solution)/shard_map/ppermute | solution.py:39
  413.3 7.4 %collective-permute-done.4 = f32[128,1024]{0,1:T(8,128)S(1)} collective-permute-done((f32[128,1024]{0,1:T(8,128)S(1)}, f32[128,1024]{0,1:T(8,128)S(1)}, u32[]{:S(2)}, u32[]{:S(2)}) %collective-permute-start.4) | collective-permute-done | bytes 524320 | tf_op jit(solution)/shard_map/ppermute | solution.py:39
  478.7 7.7 %gather_fusion = f32[16,128,1024]{1,2,0:T(8,128)} fusion(f32[16,128,1024]{1,2,0:T(8,128)} %bitcast_dynamic-update-slice_fusion.2, s32[1024]{0:T(1024)S(1)} %pad_clamp_fusion), kind=kCustom, calls=%fused_computation | custom fusion | bytes 16777280 | tf_op jit(solution)/shard_map/gather | solution.py:44
  486.4 9.3 %copy.12 = f32[16,128,1024]{2,1,0:T(8,128)} copy(f32[16,128,1024]{1,2,0:T(8,128)} %gather_fusion) | data formatting | bytes 16777216 | tf_op jit(solution)/shard_map/gather | solution.py:44
  501.8 9.2 %copy.16 = f32[2048,1024]{0,1:T(8,128)} copy(f32[2048,1024]{1,0:T(8,128)} %param.6) | data formatting | bytes 16777216 | tf_op args[2]
  511.0 59.5 %all-reduce.3.cloned.1.call-done = f32[4,256,1024]{2,1,0:T(8,128)} async-done(((f32[4,256,1024]{2,1,0:T(8,128)}), f32[4,256,1024]{2,1,0:T(8,128)}) %all-reduce.3.cloned.1.call-update) | async-done | bytes 4194320 | tf_op jit(solution)/shard_map/psum | solution.py:17
  570.5 32.5 %broadcast_multiply_fusion = f32[8,256,4,256]{3,1,2,0:T(8,128)} fusion(f32[8,4]{1,0:T(8,128)S(1)} %copy.14, f32[8,256,1024,1]{2,1,3,0:T(8,128)} %bitcast.159, f32[4,256,1024]{2,1,0:T(8,128)} %all-reduce.3.cloned.1.call-done), kind=kOutput, calls=%fused_computation.7 | convolution fusion | flops 25771900928 | bytes 20971648 | tf_op jit(solution)/shard_map/dot_general | solution.py:48
  603.0 10.6 %copy.15 = f32[8,256,4,256]{1,0,3,2:T(8,128)} copy(f32[8,256,4,256]{3,1,2,0:T(8,128)} %broadcast_multiply_fusion) | data formatting | bytes 16777216 | tf_op jit(solution)/shard_map/mul | solution.py:55
  613.6 10.7 %copy.20 = f32[128,8,8,256]{3,1,2,0:T(8,128)} copy(f32[128,8,8,256]{3,2,1,0:T(8,128)} %bitcast.157) | data formatting | bytes 16777216
  624.3 11.7 %sub.27 = f32[2048,1024]{0,1:T(8,128)} subtract(f32[2048,1024]{0,1:T(8,128)} %copy.16, f32[2048,1024]{0,1:T(8,128)} %bitcast.156) | non-fusion elementwise | flops 2097152 | bytes 25165824 | tf_op jit(solution)/shard_map/sub | solution.py:56
  636.0 9.2 %copy.18 = f32[2048,1024]{1,0:T(8,128)} copy(f32[2048,1024]{0,1:T(8,128)} %sub.27) | data formatting | bytes 16777216
  (154 shorter events, 169.9 us)
Async XLA Ops:
  7.2 563.4 %all-reduce.3.cloned.1.call-start = ((), (), s32[]{:S(2)}) async-start(), calls=%async_computation | async-start | bytes 8388608 | tf_op jit(solution)/shard_map/psum | solution.py:17
  17.0 2.0 copy-start
  222.1 108.1 %copy-start.1 = (f32[128,1024]{1,0:T(8,128)S(1)}, f32[128,1024]{1,0:T(8,128)}, u32[]{:S(2)}) copy-start(f32[128,1024]{1,0:T(8,128)} %param.5) | copy-start | bytes 1572868
  343.5 17.3 %collective-permute-start = (f32[128,1024]{0,1:T(8,128)S(1)}, f32[128,1024]{0,1:T(8,128)S(1)}, u32[]{:S(2)}, u32[]{:S(2)}) collective-permute-start(f32[128,1024]{0,1:T(8,128)S(1)} %bitcast.161), channel_id=1, source_target_pairs={{0,1},{1,2},{2,3},{3,4},{4,5},{5,6},{6,7},{7,8},{8,9},{9,10},{10,1... | collective-permute-start | bytes 1572872 | tf_op jit(solution)/shard_map/ppermute | solution.py:39
  360.8 16.4 %collective-permute-start.1 = (f32[128,1024]{0,1:T(8,128)S(1)}, f32[128,1024]{0,1:T(8,128)S(1)}, u32[]{:S(2)}, u32[]{:S(2)}) collective-permute-start(f32[128,1024]{0,1:T(8,128)S(1)} %collective-permute-done), channel_id=1, source_target_pairs={{0,1},{1,2},{2,3},{3,4},{4,5},{5,6},{6,7},{7,8},{8,9},{9,10},{10,1... | collective-permute-start | bytes 1572872 | tf_op jit(solution)/shard_map/ppermute | solution.py:39
  360.8 16.4 %collective-permute-start.8 = (f32[128,1024]{0,1:T(8,128)S(1)}, f32[128,1024]{0,1:T(8,128)S(1)}, u32[]{:S(2)}, u32[]{:S(2)}) collective-permute-start(f32[128,1024]{0,1:T(8,128)S(1)} %bitcast.162), channel_id=1, source_target_pairs={{1,0},{2,1},{3,2},{4,3},{5,4},{6,5},{7,6},{8,7},{9,8},{10,9},{11,1... | collective-permute-start | bytes 1572872 | tf_op jit(solution)/shard_map/ppermute | solution.py:41
  377.2 15.5 %collective-permute-start.2 = (f32[128,1024]{0,1:T(8,128)S(1)}, f32[128,1024]{0,1:T(8,128)S(1)}, u32[]{:S(2)}, u32[]{:S(2)}) collective-permute-start(f32[128,1024]{0,1:T(8,128)S(1)} %collective-permute-done.1), channel_id=1, source_target_pairs={{0,1},{1,2},{2,3},{3,4},{4,5},{5,6},{6,7},{7,8},{8,9},{9,10},{10,1... | collective-permute-start | bytes 1572872 | tf_op jit(solution)/shard_map/ppermute | solution.py:39
  377.2 15.5 %collective-permute-start.9 = (f32[128,1024]{0,1:T(8,128)S(1)}, f32[128,1024]{0,1:T(8,128)S(1)}, u32[]{:S(2)}, u32[]{:S(2)}) collective-permute-start(f32[128,1024]{0,1:T(8,128)S(1)} %collective-permute-done.8), channel_id=1, source_target_pairs={{1,0},{2,1},{3,2},{4,3},{5,4},{6,5},{7,6},{8,7},{9,8},{10,9},{11,1... | collective-permute-start | bytes 1572872 | tf_op jit(solution)/shard_map/ppermute | solution.py:41
  392.6 14.5 %collective-permute-start.3 = (f32[128,1024]{0,1:T(8,128)S(1)}, f32[128,1024]{0,1:T(8,128)S(1)}, u32[]{:S(2)}, u32[]{:S(2)}) collective-permute-start(f32[128,1024]{0,1:T(8,128)S(1)} %collective-permute-done.2), channel_id=1, source_target_pairs={{0,1},{1,2},{2,3},{3,4},{4,5},{5,6},{6,7},{7,8},{8,9},{9,10},{10,1... | collective-permute-start | bytes 1572872 | tf_op jit(solution)/shard_map/ppermute | solution.py:39
  392.6 14.5 %collective-permute-start.10 = (f32[128,1024]{0,1:T(8,128)S(1)}, f32[128,1024]{0,1:T(8,128)S(1)}, u32[]{:S(2)}, u32[]{:S(2)}) collective-permute-start(f32[128,1024]{0,1:T(8,128)S(1)} %collective-permute-done.9), channel_id=1, source_target_pairs={{1,0},{2,1},{3,2},{4,3},{5,4},{6,5},{7,6},{8,7},{9,8},{10,9},{11,1... | collective-permute-start | bytes 1572872 | tf_op jit(solution)/shard_map/ppermute | solution.py:41
  407.2 27.0 %copy-start.6 = (f32[128,1024]{0,1:T(8,128)}, f32[128,1024]{0,1:T(8,128)S(1)}, u32[]{:S(2)}) copy-start(f32[128,1024]{0,1:T(8,128)S(1)} %collective-permute-done.3) | copy-start | bytes 1572868
  407.2 13.6 %collective-permute-start.4 = (f32[128,1024]{0,1:T(8,128)S(1)}, f32[128,1024]{0,1:T(8,128)S(1)}, u32[]{:S(2)}, u32[]{:S(2)}) collective-permute-start(f32[128,1024]{0,1:T(8,128)S(1)} %collective-permute-done.3), channel_id=1, source_target_pairs={{0,1},{1,2},{2,3},{3,4},{4,5},{5,6},{6,7},{7,8},{8,9},{9,10},{10,1... | collective-permute-start | bytes 1572872 | tf_op jit(solution)/shard_map/ppermute | solution.py:39
  407.2 0.9 copy-start.2
  408.0 12.8 %collective-permute-start.11 = (f32[128,1024]{0,1:T(8,128)S(1)}, f32[128,1024]{0,1:T(8,128)S(1)}, u32[]{:S(2)}, u32[]{:S(2)}) collective-permute-start(f32[128,1024]{0,1:T(8,128)S(1)} %collective-permute-done.10), channel_id=1, source_target_pairs={{1,0},{2,1},{3,2},{4,3},{5,4},{6,5},{7,6},{8,7},{9,8},{10,9},{11,1... | collective-permute-start | bytes 1572872 | tf_op jit(solution)/shard_map/ppermute | solution.py:41
  420.8 19.3 %copy-start.8 = (f32[128,1024]{0,1:T(8,128)}, f32[128,1024]{0,1:T(8,128)S(1)}, u32[]{:S(2)}) copy-start(f32[128,1024]{0,1:T(8,128)S(1)} %collective-permute-done.4) | copy-start | bytes 1572868
  420.8 12.7 %collective-permute-start.5 = (f32[128,1024]{0,1:T(8,128)S(1)}, f32[128,1024]{0,1:T(8,128)S(1)}, u32[]{:S(2)}, u32[]{:S(2)}) collective-permute-start(f32[128,1024]{0,1:T(8,128)S(1)} %collective-permute-done.4), channel_id=1, source_target_pairs={{0,1},{1,2},{2,3},{3,4},{4,5},{5,6},{6,7},{7,8},{8,9},{9,10},{10,1... | collective-permute-start | bytes 1572872 | tf_op jit(solution)/shard_map/ppermute | solution.py:39
  420.8 0.9 copy-start.4
  421.7 12.4 %collective-permute-start.12 = (f32[128,1024]{0,1:T(8,128)S(1)}, f32[128,1024]{0,1:T(8,128)}, u32[]{:S(2)}, u32[]{:S(2)}) collective-permute-start(f32[128,1024]{0,1:T(8,128)S(1)} %collective-permute-done.11), channel_id=1, source_target_pairs={{1,0},{2,1},{3,2},{4,3},{5,4},{6,5},{7,6},{8,7},{9,8},{10,9},{11,1... | collective-permute-start | bytes 1572872 | tf_op jit(solution)/shard_map/ppermute | solution.py:41
  433.5 12.8 %copy-start.9 = (f32[128,1024]{0,1:T(8,128)}, f32[128,1024]{0,1:T(8,128)S(1)}, u32[]{:S(2)}) copy-start(f32[128,1024]{0,1:T(8,128)S(1)} %collective-permute-done.5) | copy-start | bytes 1572868
  433.5 12.8 %collective-permute-start.6 = (f32[128,1024]{0,1:T(8,128)S(1)}, f32[128,1024]{0,1:T(8,128)}, u32[]{:S(2)}, u32[]{:S(2)}) collective-permute-start(f32[128,1024]{0,1:T(8,128)S(1)} %collective-permute-done.5), channel_id=1, source_target_pairs={{0,1},{1,2},{2,3},{3,4},{4,5},{5,6},{6,7},{7,8},{8,9},{9,10},{10,1... | collective-permute-start | bytes 1572872 | tf_op jit(solution)/shard_map/ppermute | solution.py:39
  434.2 13.5 %collective-permute-start.13 = (f32[128,1024]{0,1:T(8,128)}, f32[128,1024]{0,1:T(8,128)}, u32[]{:S(2)}, u32[]{:S(2)}) collective-permute-start(f32[128,1024]{0,1:T(8,128)} %collective-permute-done.12), channel_id=1, source_target_pairs={{1,0},{2,1},{3,2},{4,3},{5,4},{6,5},{7,6},{8,7},{9,8},{10,9},{11,1... | collective-permute-start | bytes 1572872 | tf_op jit(solution)/shard_map/ppermute | solution.py:41
  446.3 12.8 %collective-permute-start.7 = (f32[128,1024]{0,1:T(8,128)}, f32[128,1024]{0,1:T(8,128)}, u32[]{:S(2)}, u32[]{:S(2)}) collective-permute-start(f32[128,1024]{0,1:T(8,128)} %collective-permute-done.6), channel_id=1, source_target_pairs={{0,1},{1,2},{2,3},{3,4},{4,5},{5,6},{6,7},{7,8},{8,9},{9,10},{10,1... | collective-permute-start | bytes 1572872 | tf_op jit(solution)/shard_map/ppermute | solution.py:39
  446.3 20.3 %copy-start.7 = (f32[128,1024]{0,1:T(8,128)S(1)}, f32[128,1024]{0,1:T(8,128)}, u32[]{:S(2)}) copy-start(f32[128,1024]{0,1:T(8,128)} %copy-done.6) | copy-start | bytes 1572868
  447.6 30.2 %collective-permute-start.14 = (f32[128,1024]{0,1:T(8,128)}, f32[128,1024]{0,1:T(8,128)S(1)}, u32[]{:S(2)}, u32[]{:S(2)}) collective-permute-start(f32[128,1024]{0,1:T(8,128)} %collective-permute-done.13), channel_id=1, source_target_pairs={{1,0},{2,1},{3,2},{4,3},{5,4},{6,5},{7,6},{8,7},{9,8},{10,9},{11,1... | collective-permute-start | bytes 1572872 | tf_op jit(solution)/shard_map/ppermute | solution.py:41
  464.7 7.7 %copy-start.3 = (f32[128,1024]{0,1:T(8,128)S(1)}, f32[128,1024]{0,1:T(8,128)}, u32[]{:S(2)}) copy-start(f32[128,1024]{0,1:T(8,128)} %copy-done.2) | copy-start | bytes 1572868
  466.7 6.6 %copy-start.5 = (f32[128,1024]{0,1:T(8,128)S(1)}, f32[128,1024]{0,1:T(8,128)}, u32[]{:S(2)}) copy-start(f32[128,1024]{0,1:T(8,128)} %copy-done.4) | copy-start | bytes 1572868
  500.6 1.0 copy-start.10
Sparse Core Ops, SparseCore 0:
  500.8 69.7 all-reduce.2
